TPU v7x, 32 devices: a whole 2x2x4 slice. The times are simulated.
32 devices in a mesh: ty: 4 (over y, x), tx: 8 (over z, core).
Axes of the slice: x: 2, y: 2, z: 4, core: 2. Of those that a mesh axis runs over, the one named last changes fastest.
Arguments:
- channel_cube: bfloat16 [256, 512, 128], P(('ty', 'tx'))
- footprint: int32 [32, 8], replicated, may hold values 0 or 1
- kernel_sigmas: int32 [4], replicated, may hold values from 1 to 3, as said below
- spectral_taps: int32 [2, 4], replicated, may hold values from 1 to 5, as said below
Outputs:
- snr_cubes: bfloat16 [4, 512, 128, 256], P(None, 'ty', 'tx')
Inputs may be any that keep to these rules, and one draw needn't show every extreme that they name: `kernel_sigmas`: some scale has exactly 3. `spectral_taps`: row 0 holds widths up to 5, row 1 dilations up to 4; some scale has width 5 and dilation 4 together.
All inputs are finite; a program needn't handle non-finite values.
Results may differ from a plain program's by a relative error of at most 0.0077.
Values may be sent and summed in bfloat16 or wider, within the bound.
No kernel may reach another device: no remote copies, remote signals or barrier semaphores. Data moves between devices by JAX's collectives and lax.ppermute only.
A program may use at most 192 MiB of HBM per device.

v0:
```python
import jax
import jax.numpy as jnp
from jax import lax
from jax.sharding import PartitionSpec as P

TILE_Y = 128
TILE_X = 16
NSC = 4
WMAX = 5
PT = 16
HALO = 9
PADC = 8


def with_halo(x, sides, width):
    for axis, dim in sides:
        peers, length = (lax.axis_size(axis), x.shape[dim])
        up = [(i, (i + 1) % peers) for i in range(peers - 1)]
        down = [(j, i) for i, j in up]
        last = lax.slice_in_dim(x, length - width, length, axis=dim)
        leading = lax.slice_in_dim(x, 0, width, axis=dim)
        before = lax.ppermute(last, axis, up)
        after = lax.ppermute(leading, axis, down)
        x = jnp.concatenate([before, x, after], axis=dim)
    return x


def gauss_taps(sigma_value):
    offsets = jnp.arange(-HALO, HALO + 1).astype(jnp.float32)
    spread = sigma_value.astype(jnp.float32)
    weights = jnp.exp(-offsets * offsets / (2.0 * spread * spread))
    weights = jnp.where(jnp.abs(offsets) <= 3.0 * spread, weights, jnp.float32(0.0))
    return weights / jnp.sum(weights)


def boxcar(field, width, dilation):
    last = field.ndim - 1
    channels = field.shape[last]
    pads = [(0, 0)] * last + [(PADC, PADC)]
    padded = jnp.pad(field, pads)
    total = jnp.zeros(field.shape, jnp.float32)
    for step in range(WMAX):
        start = PADC + dilation * (step - (width - 1) // 2)
        piece = lax.dynamic_slice_in_dim(padded, start, channels, last)
        total = total + jnp.where(step < width, piece, jnp.float32(0.0))
    return total / width.astype(jnp.float32)


def band_matrix(taps_bf, length):
    out_index = jnp.arange(length)[:, None, None]
    in_index = jnp.arange(length + 2 * HALO)[None, :, None]
    tap_index = jnp.arange(2 * HALO + 1)[None, None, :]
    chosen = jnp.where(
        in_index - out_index == tap_index,
        taps_bf.astype(jnp.float32)[None, None, :],
        jnp.float32(0.0),
    )
    return jnp.sum(chosen, axis=2).astype(jnp.bfloat16)


def relay(pieces):
    ch_local, n_rows, n_cols, cells = pieces.shape
    arrived = lax.all_to_all(
        pieces.reshape(ch_local, n_rows * n_cols, cells),
        ("ty", "tx"),
        split_axis=1,
        concat_axis=0,
        tiled=True,
    )
    return arrived.reshape(-1, cells)


def local(channel_cube, footprint, kernel_sigmas, spectral_taps):
    n_rows = lax.axis_size("ty")
    n_cols = lax.axis_size("tx")
    ch_local, full_y, full_x = channel_cube.shape
    pixel_mask = jnp.repeat(jnp.repeat(footprint, PT, 0), PT, 1).astype(jnp.float32)
    count = jnp.maximum(jnp.sum(pixel_mask), jnp.float32(1.0))
    row_start = lax.axis_index("ty") * TILE_Y
    col_start = lax.axis_index("tx") * TILE_X
    tile_mask = lax.dynamic_slice(pixel_mask, (row_start, col_start), (TILE_Y, TILE_X))
    plane_vals = jnp.where(
        pixel_mask[None] > 0.5, channel_cube.astype(jnp.float32), jnp.float32(0.0)
    )
    local_squares = jnp.sum(plane_vals * plane_vals, axis=(1, 2))
    squares = lax.all_gather(local_squares, ("ty", "tx"), axis=0, tiled=True)
    pieces = channel_cube.reshape(ch_local, n_rows, TILE_Y, n_cols, TILE_X).transpose(0, 1, 3, 2, 4)
    arrived = relay(pieces.reshape(ch_local, n_rows, n_cols, TILE_Y * TILE_X))
    channels = arrived.shape[0]
    tile_cells = arrived.T.reshape(TILE_Y, TILE_X, channels)
    tile_cells = jnp.where(tile_mask[:, :, None] > 0.5, tile_cells, jnp.zeros_like(tile_cells))
    padded = with_halo(tile_cells, (("ty", 0), ("tx", 1)), HALO)
    channel_noise = jnp.sqrt(squares / count + 1e-06)
    results = []
    for scale_idx in range(NSC):
        taps = gauss_taps(kernel_sigmas[scale_idx])
        taps_bf = taps.astype(jnp.bfloat16)
        row_band = band_matrix(taps_bf, TILE_Y)
        col_band = band_matrix(taps_bf, TILE_X)
        rows_pass = jnp.einsum(
            "ij,jxc->ixc", row_band, padded, preferred_element_type=jnp.float32
        ).astype(jnp.bfloat16)
        smooth = jnp.einsum("xk,ykc->yxc", col_band, rows_pass, preferred_element_type=jnp.float32)
        width = spectral_taps[0, scale_idx]
        dilation = spectral_taps[1, scale_idx]
        boxed = boxcar(smooth, width, dilation)
        knorm = jnp.sum(taps * taps) / jnp.sqrt(width.astype(jnp.float32))
        scaled = boxed * tile_mask[:, :, None] / (channel_noise[None, None, :] * knorm)
        results.append(scaled.astype(jnp.bfloat16))
    return jnp.stack(results)


def solution(mesh):
    placed = (P(("ty", "tx"), None, None), P(), P(), P())
    return jax.shard_map(
        local, mesh=mesh, in_specs=placed, out_specs=P(None, "ty", "tx", None), check_vma=False
    )
```

profile of v0, /device:TPU:3, one launch (start us, length us, event | category | flops | bytes accessed | tf_op | source)
XLA Modules:
  0.0 176.3 jit_solution(6123437555780068440)
XLA Ops:
  0.0 1.5 copy.34
  1.5 0.3 reshape.161
  1.8 5.8 %copy.45 = bf16[8,4,8,128,16]{4,3,0,2,1:T(8,128)(2,1)} copy(bf16[8,4,8,128,16]{3,1,4,2,0:T(4,128)(2,1)S(1)} %bitcast.95) | data formatting | bytes 2097152 | tf_op jit(solution)/shard_map/reshape;reshape | solution.py:64
  7.5 15.8 %reshape.174 = bf16[8,32,2048]{2,0,1:T(8,128)(2,1)} reshape(bf16[8,4,8,128,16]{4,3,0,2,1:T(8,128)(2,1)} %copy.45) | data formatting | bytes 2097152 | tf_op jit(solution)/shard_map/reshape;reshape | solution.py:64
  23.3 0.0 copy-start.2
  23.3 0.0 copy-start.1
  23.3 0.0 copy-start.3
  23.3 0.0 copy-start
  23.4 6.4 %all-to-all-start = ((bf16[8,32,2048]{2,0,1:T(8,128)(2,1)}), bf16[8,32,2048]{2,0,1:T(8,128)(2,1)S(1)}, u32[]{:S(2)}, u32[]{:S(2)}) async-start(bf16[8,32,2048]{2,0,1:T(8,128)(2,1)} %reshape.174), calls=%async_computation | async-start | bytes 2097152 | tf_op jit(solution)/shard_map/all_to_all | solution.py:63
  29.8 0.0 copy-done.2
  29.8 0.7 fusion.87
  33.1 0.0 copy-done.1
  33.1 0.7 fusion.86
  64.1 0.0 copy-done.3
  64.2 0.1 broadcast_in_dim.164
  64.3 0.1 convert_element_type.227
  64.5 0.2 copy.41
  64.7 0.1 copy.40
  65.1 0.7 fusion.80
  65.7 1.3 multiply_reduce_fusion.4
  67.6 0.7 broadcast_reduce_fusion
  69.0 0.6 fusion.81
  69.6 1.2 multiply_reduce_fusion.3
  71.4 0.6 fusion.82
  72.1 1.3 multiply_reduce_fusion.2
  74.0 0.7 fusion.83
  74.7 1.4 multiply_reduce_fusion.1
  76.8 0.0 copy-done
  76.8 0.5 multiply_reduce_fusion
  77.3 0.2 dynamic-update-slice
  77.5 38.9 %all-reduce.4 = f32[256]{0:T(256)S(1)} all-reduce(f32[256]{0:T(256)S(1)} %dynamic-update-slice), channel_id=1, replica_groups=mesh['ty'=4,'tx'=8] {'ty','tx'}, use_global_device_ids=true, to_apply=%add.4 | all-reduce | flops 256 | bytes 2048
  116.4 1.3 convert_convert_fusion
  117.7 1.3 convert_convert_fusion.2
  119.0 0.1 select_reduce_fusion.7
  119.1 0.0 all-to-all-done
  119.1 0.5 copy.37
  119.7 0.7 copy_select_fusion
  120.5 3.1 %collective-permute-start = (bf16[9,16,256]{2,0,1:T(8,128)(2,1)S(1)}, bf16[9,16,256]{2,0,1:T(8,128)(2,1)S(1)}, u32[]{:S(2)}, u32[]{:S(2)}) collective-permute-start(bf16[9,16,256]{2,0,1:T(8,128)(2,1)S(1)} %get-tuple-element.19), channel_id=1, source_target_pairs={{0,8},{8,16},{16,24},{1,9},{9,17},{17,25},{2,10},{10,18},{18,26},{... | collective-permute-start | bytes 221192 | tf_op jit(solution)/shard_map/ppermute | solution.py:22
  123.6 2.2 %collective-permute-start.1 = (bf16[9,16,256]{2,0,1:T(8,128)(2,1)S(1)}, bf16[9,16,256]{2,0,1:T(8,128)(2,1)S(1)}, u32[]{:S(2)}, u32[]{:S(2)}) collective-permute-start(bf16[9,16,256]{2,0,1:T(8,128)(2,1)S(1)} %get-tuple-element.20), channel_id=1, source_target_pairs={{8,0},{16,8},{24,16},{9,1},{17,9},{25,17},{10,2},{18,10},{26,18},{... | collective-permute-start | bytes 221192 | tf_op jit(solution)/shard_map/ppermute | solution.py:23
  125.8 0.4 collective-permute-done
  126.2 4.3 %collective-permute-done.1 = bf16[9,16,256]{2,0,1:T(8,128)(2,1)S(1)} collective-permute-done((bf16[9,16,256]{2,0,1:T(8,128)(2,1)S(1)}, bf16[9,16,256]{2,0,1:T(8,128)(2,1)S(1)}, u32[]{:S(2)}, u32[]{:S(2)}) %collective-permute-start.1) | collective-permute-done | bytes 73760 | tf_op jit(solution)/shard_map/ppermute | solution.py:23
  130.4 0.5 pad_maximum_fusion.2
  130.9 0.1 fusion.84
  131.0 6.6 %collective-permute-start.2 = (bf16[146,9,256]{2,0,1:T(8,128)(2,1)S(1)}, bf16[146,9,256]{2,0,1:T(8,128)(2,1)S(1)}, u32[]{:S(2)}, u32[]{:S(2)}) collective-permute-start(bf16[146,9,256]{2,0,1:T(8,128)(2,1)S(1)} %get-tuple-element.17), channel_id=1, source_target_pairs={{0,1},{1,2},{2,3},{3,4},{4,5},{5,6},{6,7},{8,9},{9,10},{10,11},{11... | collective-permute-start | bytes 2018312 | tf_op jit(solution)/shard_map/ppermute | solution.py:22
  137.6 2.1 %collective-permute-start.3 = (bf16[146,9,256]{2,0,1:T(8,128)(2,1)S(1)}, bf16[146,9,256]{2,0,1:T(8,128)(2,1)S(1)}, u32[]{:S(2)}, u32[]{:S(2)}) collective-permute-start(bf16[146,9,256]{2,0,1:T(8,128)(2,1)S(1)} %get-tuple-element.18), channel_id=1, source_target_pairs={{1,0},{2,1},{3,2},{4,3},{5,4},{6,5},{7,6},{9,8},{10,9},{11,10},{12... | collective-permute-start | bytes 2018312 | tf_op jit(solution)/shard_map/ppermute | solution.py:23
  139.8 0.8 select_reduce_fusion.3
  140.6 5.0 %collective-permute-done.2 = bf16[146,9,256]{2,0,1:T(8,128)(2,1)S(1)} collective-permute-done((bf16[146,9,256]{2,0,1:T(8,128)(2,1)S(1)}, bf16[146,9,256]{2,0,1:T(8,128)(2,1)S(1)}, u32[]{:S(2)}, u32[]{:S(2)}) %collective-permute-start.2) | collective-permute-done | bytes 672800 | tf_op jit(solution)/shard_map/ppermute | solution.py:22
  145.6 4.4 %collective-permute-done.3 = bf16[146,9,256]{2,0,1:T(8,128)(2,1)S(1)} collective-permute-done((bf16[146,9,256]{2,0,1:T(8,128)(2,1)S(1)}, bf16[146,9,256]{2,0,1:T(8,128)(2,1)S(1)}, u32[]{:S(2)}, u32[]{:S(2)}) %collective-permute-start.3) | collective-permute-done | bytes 672800 | tf_op jit(solution)/shard_map/ppermute | solution.py:23
  150.0 1.2 convolution_convert_fusion.3
  151.3 1.3 fusion.48
  152.6 1.2 convolution_convert_fusion.2
  153.9 1.3 fusion.51
  155.2 1.2 convolution_convert_fusion.1
  156.5 1.3 fusion.54
  157.8 1.2 convolution_convert_fusion
  159.0 1.3 fusion.57
  160.4 3.2 %fusion.60 = bf16[1,128,16,256]{3,2,1,0:T(8,128)(2,1)S(1)} fusion(f32[256]{0:T(256)S(1)} %get-tuple-element.13, f32[128,16]{1,0:T(8,128)S(1)} %copy.40, f32[]{:T(128)} %bitcast.18, s32[]{:T(128)S(6)} %select_n.301, f32[128,16,256]{2,1,0:T(8,128)S(1)} %fusion.48, pred[]{:T(512)} %bitcast.17, s32[]{:T(128)S(6)} %select_n.298, pred[]{:T(512)} %bitcast.16, ...), kind=kLoop, calls=%fused_computation.90 | loop fusion | flops 6815744 | bytes 3154973 | tf_op jit(solution)/shard_map/stack | solution.py:110
  163.6 3.4 %fusion.61 = bf16[1,128,16,256]{3,2,1,0:T(8,128)(2,1)S(1)} fusion(f32[256]{0:T(256)S(1)} %get-tuple-element.29, f32[128,16]{1,0:T(8,128)S(1)} %copy.40, f32[]{:T(128)} %bitcast.31, s32[]{:T(128)S(6)} %select_n.321, f32[128,16,256]{2,1,0:T(8,128)S(1)} %fusion.51, pred[]{:T(512)} %bitcast.30, s32[]{:T(128)S(6)} %select_n.318, pred[]{:T(512)} %bitcast.29, ...), kind=kLoop, calls=%fused_computation.91 | loop fusion | flops 6815744 | bytes 3154973 | tf_op jit(solution)/shard_map/stack | solution.py:110
  167.0 3.6 %fusion.62 = bf16[1,128,16,256]{3,2,1,0:T(8,128)(2,1)S(1)} fusion(f32[256]{0:T(256)S(1)} %get-tuple-element.30, f32[128,16]{1,0:T(8,128)S(1)} %copy.40, f32[]{:T(128)} %bitcast.44, s32[]{:T(128)S(6)} %select_n.340, f32[128,16,256]{2,1,0:T(8,128)S(1)} %fusion.54, pred[]{:T(512)} %bitcast.43, s32[]{:T(128)S(6)} %select_n.337, pred[]{:T(512)} %bitcast.42, ...), kind=kLoop, calls=%fused_computation.92 | loop fusion | flops 6815744 | bytes 3154973 | tf_op jit(solution)/shard_map/stack | solution.py:110
  170.6 3.4 %fusion.63 = bf16[1,128,16,256]{3,2,1,0:T(8,128)(2,1)S(1)} fusion(f32[256]{0:T(256)S(1)} %get-tuple-element.31, f32[128,16]{1,0:T(8,128)S(1)} %copy.40, f32[]{:T(128)} %bitcast.57, s32[]{:T(128)S(6)} %select_n.359, f32[128,16,256]{2,1,0:T(8,128)S(1)} %fusion.57, pred[]{:T(512)} %bitcast.56, s32[]{:T(128)S(6)} %select_n.356, pred[]{:T(512)} %bitcast.55, ...), kind=kLoop, calls=%fused_computation.93 | loop fusion | flops 6815744 | bytes 3154973 | tf_op jit(solution)/shard_map/stack | solution.py:110
  174.0 2.3 %pad_maximum_fusion = bf16[4,128,16,256]{3,2,1,0:T(8,128)(2,1)} fusion(bf16[1,128,16,256]{3,2,1,0:T(8,128)(2,1)S(1)} %fusion.63, bf16[1,128,16,256]{3,2,1,0:T(8,128)(2,1)S(1)} %fusion.62, bf16[1,128,16,256]{3,2,1,0:T(8,128)(2,1)S(1)} %fusion.61, bf16[1,128,16,256]{3,2,1,0:T(8,128)(2,1)S(1)} %fusion.60), kind=kLoop, calls=%fused_computation.20 | loop fusion | flops 6291456 | bytes 8388608 | tf_op jit(solution)/shard_map/stack | solution.py:110
  (10 shorter events, 0.1 us)
Async XLA Ops:
  23.3 6.4 %copy-start.2 = (s32[4]{0:T(128)S(1)}, s32[4]{0:T(128)}, u32[]{:S(2)}) copy-start(s32[4]{0:T(128)} %param.6) | copy-start | bytes 52
  23.3 9.8 %copy-start.1 = (s32[2,4]{1,0:T(2,128)S(1)}, s32[2,4]{1,0:T(2,128)}, u32[]{:S(2)}) copy-start(s32[2,4]{1,0:T(2,128)} %param.7) | copy-start | bytes 100
  23.3 40.8 %copy-start.3 = (s32[32,8]{0,1:T(8,128)S(1)}, s32[32,8]{0,1:T(8,128)}, u32[]{:S(2)}) copy-start(s32[32,8]{0,1:T(8,128)} %param.5) | copy-start | bytes 3076
  23.3 53.5 %copy-start = (bf16[8,512,128]{2,1,0:T(8,128)(2,1)S(1)}, bf16[8,512,128]{2,1,0:T(8,128)(2,1)}, u32[]{:S(2)}) copy-start(bf16[8,512,128]{2,1,0:T(8,128)(2,1)} %param.4) | copy-start | bytes 3145732
  23.4 95.8 %all-to-all-start = ((bf16[8,32,2048]{2,0,1:T(8,128)(2,1)}), bf16[8,32,2048]{2,0,1:T(8,128)(2,1)S(1)}, u32[]{:S(2)}, u32[]{:S(2)}) async-start(bf16[8,32,2048]{2,0,1:T(8,128)(2,1)} %reshape.174), calls=%async_computation | async-start | bytes 2097152 | tf_op jit(solution)/shard_map/all_to_all | solution.py:63
  120.5 5.7 %collective-permute-start = (bf16[9,16,256]{2,0,1:T(8,128)(2,1)S(1)}, bf16[9,16,256]{2,0,1:T(8,128)(2,1)S(1)}, u32[]{:S(2)}, u32[]{:S(2)}) collective-permute-start(bf16[9,16,256]{2,0,1:T(8,128)(2,1)S(1)} %get-tuple-element.19), channel_id=1, source_target_pairs={{0,8},{8,16},{16,24},{1,9},{9,17},{17,25},{2,10},{10,18},{18,26},{... | collective-permute-start | bytes 221192 | tf_op jit(solution)/shard_map/ppermute | solution.py:22
  123.6 6.9 %collective-permute-start.1 = (bf16[9,16,256]{2,0,1:T(8,128)(2,1)S(1)}, bf16[9,16,256]{2,0,1:T(8,128)(2,1)S(1)}, u32[]{:S(2)}, u32[]{:S(2)}) collective-permute-start(bf16[9,16,256]{2,0,1:T(8,128)(2,1)S(1)} %get-tuple-element.20), channel_id=1, source_target_pairs={{8,0},{16,8},{24,16},{9,1},{17,9},{25,17},{10,2},{18,10},{26,18},{... | collective-permute-start | bytes 221192 | tf_op jit(solution)/shard_map/ppermute | solution.py:23
  131.0 14.6 %collective-permute-start.2 = (bf16[146,9,256]{2,0,1:T(8,128)(2,1)S(1)}, bf16[146,9,256]{2,0,1:T(8,128)(2,1)S(1)}, u32[]{:S(2)}, u32[]{:S(2)}) collective-permute-start(bf16[146,9,256]{2,0,1:T(8,128)(2,1)S(1)} %get-tuple-element.17), channel_id=1, source_target_pairs={{0,1},{1,2},{2,3},{3,4},{4,5},{5,6},{6,7},{8,9},{9,10},{10,11},{11... | collective-permute-start | bytes 2018312 | tf_op jit(solution)/shard_map/ppermute | solution.py:22
  137.6 12.4 %collective-permute-start.3 = (bf16[146,9,256]{2,0,1:T(8,128)(2,1)S(1)}, bf16[146,9,256]{2,0,1:T(8,128)(2,1)S(1)}, u32[]{:S(2)}, u32[]{:S(2)}) collective-permute-start(bf16[146,9,256]{2,0,1:T(8,128)(2,1)S(1)} %get-tuple-element.18), channel_id=1, source_target_pairs={{1,0},{2,1},{3,2},{4,3},{5,4},{6,5},{7,6},{9,8},{10,9},{11,10},{12... | collective-permute-start | bytes 2018312 | tf_op jit(solution)/shard_map/ppermute | solution.py:23
where the time goes:
time: 177 us; the launch traced here: 176 us
  blocking collectives  38.9 us (22%)
  between operations  37 us (21%)
  other arithmetic  29.6 us (17%)
  local copies, waits for them, and re-layouts  26 us (15%)
  starting transfers between devices  20.4 us (12%)
  waiting for transfers between devices  14.1 us (8%)
  matrix products  10.3 us (6%)
    unnamed x1, blocking collectives  38.9 us
    another operation x2, local copies, waits for them, and re-layouts, relay(): pieces.reshape(ch_local, n_rows * n_cols, cells)  21.6 us
    another operation x5, other arithmetic, local(): return jnp.stack(results)  15.9 us
    ppermute x2, starting transfers between devices, with_halo(): before = lax.ppermute(last, axis, up)  9.7 us
    ppermute x2, waiting for transfers between devices, with_halo(): after = lax.ppermute(leading, axis, down)  8.65 us
    all_to_all x1, starting transfers between devices, relay(): lax.all_to_all(pieces.reshape(ch_local, n_rows * n_cols, cells), ('ty', '...  6.41 us
    ppermute x2, waiting for transfers between devices, with_halo(): before = lax.ppermute(last, axis, up)  5.4 us
    dot_general x4, matrix products, local(): jnp.einsum('xk,ykc->yxc', col_band, rows_pass, preferred_element_type=jnp...  5.34 us
  transfers between devices with their start and end apart: 5, of which 4 were waited for; matrix products, arithmetic and copies ran while one was open for 8% of the time, Pallas kernels for 0%

commit v1 on v0

--- a/solution.py
+++ b/solution.py
@@ -60,12 +60,20 @@
 
 def relay(pieces):
     ch_local, n_rows, n_cols, cells = pieces.shape
-    arrived = lax.all_to_all(
-        pieces.reshape(ch_local, n_rows * n_cols, cells),
-        ("ty", "tx"),
-        split_axis=1,
-        concat_axis=0,
-        tiled=True,
+    arrived = jnp.concatenate(
+        lax.all_to_all(
+            jnp.stack(
+                jnp.split(
+                    pieces.reshape(ch_local, n_rows * n_cols, cells),
+                    lax.axis_size(("ty", "tx")),
+                    axis=1,
+                )
+            ),
+            ("ty", "tx"),
+            0,
+            0,
+        ),
+        axis=0,
     )
     return arrived.reshape(-1, cells)
 

time: 177 us -> 199 us (1.12)
  local copies, waits for them, and re-layouts: 26 us -> 48.1 us
    unnamed x11 -> x42, local copies, waits for them, and re-layouts: 1.68 us -> 21.5 us
    another operation x2 -> x1, local copies, waits for them, and re-layouts: 21.6 us -> 15.1 us  [relay(): pieces.reshape(ch_local, n_rows * n_cols, cells)]
    transpose x0 -> x1, local copies, waits for them, and re-layouts: none -> 5.88 us  [local(): channel_cube.reshape(ch_local, n_rows, TILE_Y, n_cols, TILE_X)]
    split x0 -> x2, local copies, waits for them, and re-layouts: none -> 2.24 us  [relay(): jnp.split(pieces.reshape(ch_local, n_rows * n_cols, cells), lax.axis_size...]
  transfers between devices with their start and end apart: 5 -> 5, of which waited for: 4 -> 4; matrix products, arithmetic and copies ran while one was open for 8% -> 7% of each run, Pallas kernels for 0% -> 0%
where the time goes in v1:
time: 199 us; the launch traced here: 198 us
  local copies, waits for them, and re-layouts  48.1 us (24%)
  blocking collectives  38.9 us (20%)
  between operations  37 us (19%)
  other arithmetic  29.6 us (15%)
  starting transfers between devices  20.4 us (10%)
  waiting for transfers between devices  14.1 us (7%)
  matrix products  10.3 us (5%)
    unnamed x1, blocking collectives  38.9 us
    unnamed x42, local copies, waits for them, and re-layouts  21.5 us
    another operation x5, other arithmetic, local(): return jnp.stack(results)  15.9 us
    another operation x1, local copies, waits for them, and re-layouts, relay(): pieces.reshape(ch_local, n_rows * n_cols, cells)  15.1 us
    ppermute x2, starting transfers between devices, with_halo(): before = lax.ppermute(last, axis, up)  9.7 us
    ppermute x2, waiting for transfers between devices, with_halo(): after = lax.ppermute(leading, axis, down)  8.65 us
    all_to_all x1, starting transfers between devices, relay(): lax.all_to_all(jnp.stack(jnp.split(pieces.reshape(ch_local, n_rows * n_co...  6.41 us
    transpose x1, local copies, waits for them, and re-layouts, local(): channel_cube.reshape(ch_local, n_rows, TILE_Y, n_cols, TILE_X)  5.88 us
  transfers between devices with their start and end apart: 5, of which 4 were waited for; matrix products, arithmetic and copies ran while one was open for 7% of the time, Pallas kernels for 0%

profile of v1, /device:TPU:3, one launch (start us, length us, event | category | flops | bytes accessed | tf_op | source)
XLA Modules:
  0.0 198.4 jit_solution(13048434863045019054)
XLA Ops:
  0.0 1.5 copy.807
  1.8 5.9 %copy.808 = bf16[8,4,8,128,16]{4,3,2,1,0:T(8,128)(2,1)} copy(bf16[8,4,8,128,16]{3,1,4,2,0:T(4,128)(2,1)S(1)} %bitcast.153) | data formatting | bytes 2097152 | tf_op jit(solution)/shard_map/transpose | solution.py:95
  7.7 15.1 %reshape_reshape.6 = bf16[8,32,2048]{2,1,0:T(8,128)(2,1)S(1)} reshape(bf16[8,4,8,128,16]{4,3,2,1,0:T(8,128)(2,1)} %copy.808) | data formatting | bytes 2097152 | tf_op jit(solution)/shard_map/reshape;reshape | solution.py:67
  22.8 0.9 fusion.87
  23.7 1.4 fusion.86
  25.1 0.6 constant_dynamic-update-slice_fusion.31
  25.7 0.6 constant_dynamic-update-slice_fusion.30
  26.3 0.6 constant_dynamic-update-slice_fusion.29
  27.0 0.6 constant_dynamic-update-slice_fusion.28
  27.6 0.6 constant_dynamic-update-slice_fusion.27
  28.2 0.6 constant_dynamic-update-slice_fusion.26
  28.9 0.6 constant_dynamic-update-slice_fusion.25
  29.5 0.6 constant_dynamic-update-slice_fusion.24
  30.2 0.6 constant_dynamic-update-slice_fusion.23
  30.8 0.6 constant_dynamic-update-slice_fusion.22
  31.4 0.6 constant_dynamic-update-slice_fusion.21
  32.7 0.6 constant_dynamic-update-slice_fusion.19
  33.4 0.6 constant_dynamic-update-slice_fusion.18
  34.0 0.6 constant_dynamic-update-slice_fusion.17
  34.6 0.6 constant_dynamic-update-slice_fusion.16
  35.3 0.6 constant_dynamic-update-slice_fusion.15
  39.1 0.6 constant_dynamic-update-slice_fusion.9
  39.7 0.6 constant_dynamic-update-slice_fusion.8
  40.4 0.6 constant_dynamic-update-slice_fusion.7
  41.0 0.6 constant_dynamic-update-slice_fusion.6
  41.7 0.6 constant_dynamic-update-slice_fusion.5
  42.3 0.6 constant_dynamic-update-slice_fusion.4
  42.9 0.6 constant_dynamic-update-slice_fusion.3
  43.6 0.6 constant_dynamic-update-slice_fusion.2
  45.5 6.4 %all-to-all-start = ((bf16[32,8,1,2048]{3,1,2,0:T(8,128)(2,1)}), bf16[32,8,1,2048]{3,1,2,0:T(8,128)(2,1)S(1)}, u32[]{:S(2)}, u32[]{:S(2)}) async-start(bf16[32,8,1,2048]{3,1,2,0:T(8,128)(2,1)} %constant_dynamic-update-slice_fusion), calls=%async_computation | async-start | bytes 2097152 | tf_op jit(solution)/shard_map/all_to_all | solution.py:64
  51.9 0.7 fusion.89
  55.3 0.7 fusion.88
  87.2 0.7 fusion.80
  87.9 1.3 multiply_reduce_fusion.4
  89.8 0.7 broadcast_reduce_fusion
  91.8 1.2 multiply_reduce_fusion.3
  94.2 1.3 multiply_reduce_fusion.2
  96.1 0.7 fusion.83
  96.8 1.4 multiply_reduce_fusion.1
  99.6 38.9 %all-reduce.4 = f32[256]{0:T(256)S(1)} all-reduce(f32[256]{0:T(256)S(1)} %dynamic-update-slice), channel_id=1, replica_groups=mesh['ty'=4,'tx'=8] {'ty','tx'}, use_global_device_ids=true, to_apply=%add.4 | all-reduce | flops 256 | bytes 2048
  138.5 1.3 convert_convert_fusion
  139.8 1.3 convert_convert_fusion.2
  141.8 0.7 copy_select_fusion
  142.6 3.1 %collective-permute-start = (bf16[9,16,256]{2,0,1:T(8,128)(2,1)S(1)}, bf16[9,16,256]{2,0,1:T(8,128)(2,1)S(1)}, u32[]{:S(2)}, u32[]{:S(2)}) collective-permute-start(bf16[9,16,256]{2,0,1:T(8,128)(2,1)S(1)} %get-tuple-element.19), channel_id=1, source_target_pairs={{0,8},{8,16},{16,24},{1,9},{9,17},{17,25},{2,10},{10,18},{18,26},{... | collective-permute-start | bytes 221192 | tf_op jit(solution)/shard_map/ppermute | solution.py:22
  145.7 2.2 %collective-permute-start.1 = (bf16[9,16,256]{2,0,1:T(8,128)(2,1)S(1)}, bf16[9,16,256]{2,0,1:T(8,128)(2,1)S(1)}, u32[]{:S(2)}, u32[]{:S(2)}) collective-permute-start(bf16[9,16,256]{2,0,1:T(8,128)(2,1)S(1)} %get-tuple-element.20), channel_id=1, source_target_pairs={{8,0},{16,8},{24,16},{9,1},{17,9},{25,17},{10,2},{18,10},{26,18},{... | collective-permute-start | bytes 221192 | tf_op jit(solution)/shard_map/ppermute | solution.py:23
  148.3 4.3 %collective-permute-done.1 = bf16[9,16,256]{2,0,1:T(8,128)(2,1)S(1)} collective-permute-done((bf16[9,16,256]{2,0,1:T(8,128)(2,1)S(1)}, bf16[9,16,256]{2,0,1:T(8,128)(2,1)S(1)}, u32[]{:S(2)}, u32[]{:S(2)}) %collective-permute-start.1) | collective-permute-done | bytes 73760 | tf_op jit(solution)/shard_map/ppermute | solution.py:23
  153.2 6.6 %collective-permute-start.2 = (bf16[146,9,256]{2,0,1:T(8,128)(2,1)S(1)}, bf16[146,9,256]{2,0,1:T(8,128)(2,1)S(1)}, u32[]{:S(2)}, u32[]{:S(2)}) collective-permute-start(bf16[146,9,256]{2,0,1:T(8,128)(2,1)S(1)} %get-tuple-element.17), channel_id=1, source_target_pairs={{0,1},{1,2},{2,3},{3,4},{4,5},{5,6},{6,7},{8,9},{9,10},{10,11},{11... | collective-permute-start | bytes 2018312 | tf_op jit(solution)/shard_map/ppermute | solution.py:22
  159.8 2.1 %collective-permute-start.3 = (bf16[146,9,256]{2,0,1:T(8,128)(2,1)S(1)}, bf16[146,9,256]{2,0,1:T(8,128)(2,1)S(1)}, u32[]{:S(2)}, u32[]{:S(2)}) collective-permute-start(bf16[146,9,256]{2,0,1:T(8,128)(2,1)S(1)} %get-tuple-element.18), channel_id=1, source_target_pairs={{1,0},{2,1},{3,2},{4,3},{5,4},{6,5},{7,6},{9,8},{10,9},{11,10},{12... | collective-permute-start | bytes 2018312 | tf_op jit(solution)/shard_map/ppermute | solution.py:23
  161.9 0.8 select_reduce_fusion.3
  162.8 5.0 %collective-permute-done.2 = bf16[146,9,256]{2,0,1:T(8,128)(2,1)S(1)} collective-permute-done((bf16[146,9,256]{2,0,1:T(8,128)(2,1)S(1)}, bf16[146,9,256]{2,0,1:T(8,128)(2,1)S(1)}, u32[]{:S(2)}, u32[]{:S(2)}) %collective-permute-start.2) | collective-permute-done | bytes 672800 | tf_op jit(solution)/shard_map/ppermute | solution.py:22
  167.8 4.4 %collective-permute-done.3 = bf16[146,9,256]{2,0,1:T(8,128)(2,1)S(1)} collective-permute-done((bf16[146,9,256]{2,0,1:T(8,128)(2,1)S(1)}, bf16[146,9,256]{2,0,1:T(8,128)(2,1)S(1)}, u32[]{:S(2)}, u32[]{:S(2)}) %collective-permute-start.3) | collective-permute-done | bytes 672800 | tf_op jit(solution)/shard_map/ppermute | solution.py:23
  172.2 1.2 convolution_convert_fusion.3
  173.4 1.3 fusion.48
  174.7 1.2 convolution_convert_fusion.2
  176.0 1.3 fusion.51
  177.3 1.2 convolution_convert_fusion.1
  178.5 1.3 fusion.54
  179.9 1.2 convolution_convert_fusion
  181.1 1.3 fusion.57
  182.5 3.2 %fusion.60 = bf16[1,128,16,256]{3,2,1,0:T(8,128)(2,1)S(1)} fusion(f32[256]{0:T(256)S(1)} %get-tuple-element.13, f32[128,16]{1,0:T(8,128)S(1)} %copy.812, f32[]{:T(128)} %bitcast.16, s32[]{:T(128)S(6)} %select_n.301, f32[128,16,256]{2,1,0:T(8,128)S(1)} %fusion.48, pred[]{:T(512)} %bitcast.15, s32[]{:T(128)S(6)} %select_n.298, pred[]{:T(512)} %bitcast.14, ...), kind=kLoop, calls=%fused_computation.90 | loop fusion | flops 6815744 | bytes 3154973 | tf_op jit(solution)/shard_map/stack | solution.py:118
  185.7 3.4 %fusion.61 = bf16[1,128,16,256]{3,2,1,0:T(8,128)(2,1)S(1)} fusion(f32[256]{0:T(256)S(1)} %get-tuple-element.61, f32[128,16]{1,0:T(8,128)S(1)} %copy.812, f32[]{:T(128)} %bitcast.29, s32[]{:T(128)S(6)} %select_n.321, f32[128,16,256]{2,1,0:T(8,128)S(1)} %fusion.51, pred[]{:T(512)} %bitcast.28, s32[]{:T(128)S(6)} %select_n.318, pred[]{:T(512)} %bitcast.27, ...), kind=kLoop, calls=%fused_computation.91 | loop fusion | flops 6815744 | bytes 3154973 | tf_op jit(solution)/shard_map/stack | solution.py:118
  189.1 3.6 %fusion.62 = bf16[1,128,16,256]{3,2,1,0:T(8,128)(2,1)S(1)} fusion(f32[256]{0:T(256)S(1)} %get-tuple-element.62, f32[128,16]{1,0:T(8,128)S(1)} %copy.812, f32[]{:T(128)} %bitcast.42, s32[]{:T(128)S(6)} %select_n.340, f32[128,16,256]{2,1,0:T(8,128)S(1)} %fusion.54, pred[]{:T(512)} %bitcast.41, s32[]{:T(128)S(6)} %select_n.337, pred[]{:T(512)} %bitcast.40, ...), kind=kLoop, calls=%fused_computation.92 | loop fusion | flops 6815744 | bytes 3154973 | tf_op jit(solution)/shard_map/stack | solution.py:118
  192.7 3.4 %fusion.63 = bf16[1,128,16,256]{3,2,1,0:T(8,128)(2,1)S(1)} fusion(f32[256]{0:T(256)S(1)} %get-tuple-element.63, f32[128,16]{1,0:T(8,128)S(1)} %copy.812, f32[]{:T(128)} %bitcast.55, s32[]{:T(128)S(6)} %select_n.359, f32[128,16,256]{2,1,0:T(8,128)S(1)} %fusion.57, pred[]{:T(512)} %bitcast.54, s32[]{:T(128)S(6)} %select_n.356, pred[]{:T(512)} %bitcast.53, ...), kind=kLoop, calls=%fused_computation.93 | loop fusion | flops 6815744 | bytes 3154973 | tf_op jit(solution)/shard_map/stack | solution.py:118
  196.1 2.3 %pad_maximum_fusion = bf16[4,128,16,256]{3,2,1,0:T(8,128)(2,1)} fusion(bf16[1,128,16,256]{3,2,1,0:T(8,128)(2,1)S(1)} %fusion.63, bf16[1,128,16,256]{3,2,1,0:T(8,128)(2,1)S(1)} %fusion.62, bf16[1,128,16,256]{3,2,1,0:T(8,128)(2,1)S(1)} %fusion.61, bf16[1,128,16,256]{3,2,1,0:T(8,128)(2,1)S(1)} %fusion.60), kind=kLoop, calls=%fused_computation.20 | loop fusion | flops 6291456 | bytes 8388608 | tf_op jit(solution)/shard_map/stack | solution.py:118
  (41 shorter events, 9.6 us)
Async XLA Ops:
  32.1 19.8 %copy-start.2 = (s32[4]{0:T(128)S(1)}, s32[4]{0:T(128)}, u32[]{:S(2)}) copy-start(s32[4]{0:T(128)} %param.6) | copy-start | bytes 52
  32.7 22.5 %copy-start.1 = (s32[2,4]{1,0:T(2,128)S(1)}, s32[2,4]{1,0:T(2,128)}, u32[]{:S(2)}) copy-start(s32[2,4]{1,0:T(2,128)} %param.7) | copy-start | bytes 100
  34.6 51.6 %copy-start.3 = (s32[32,8]{0,1:T(8,128)S(1)}, s32[32,8]{0,1:T(8,128)}, u32[]{:S(2)}) copy-start(s32[32,8]{0,1:T(8,128)} %param.5) | copy-start | bytes 3076
  41.7 57.3 %copy-start = (bf16[8,512,128]{2,1,0:T(8,128)(2,1)S(1)}, bf16[8,512,128]{2,1,0:T(8,128)(2,1)}, u32[]{:S(2)}) copy-start(bf16[8,512,128]{2,1,0:T(8,128)(2,1)} %param.4) | copy-start | bytes 3145732
  45.5 95.8 %all-to-all-start = ((bf16[32,8,1,2048]{3,1,2,0:T(8,128)(2,1)}), bf16[32,8,1,2048]{3,1,2,0:T(8,128)(2,1)S(1)}, u32[]{:S(2)}, u32[]{:S(2)}) async-start(bf16[32,8,1,2048]{3,1,2,0:T(8,128)(2,1)} %constant_dynamic-update-slice_fusion), calls=%async_computation | async-start | bytes 2097152 | tf_op jit(solution)/shard_map/all_to_all | solution.py:64
  142.6 5.7 %collective-permute-start = (bf16[9,16,256]{2,0,1:T(8,128)(2,1)S(1)}, bf16[9,16,256]{2,0,1:T(8,128)(2,1)S(1)}, u32[]{:S(2)}, u32[]{:S(2)}) collective-permute-start(bf16[9,16,256]{2,0,1:T(8,128)(2,1)S(1)} %get-tuple-element.19), channel_id=1, source_target_pairs={{0,8},{8,16},{16,24},{1,9},{9,17},{17,25},{2,10},{10,18},{18,26},{... | collective-permute-start | bytes 221192 | tf_op jit(solution)/shard_map/ppermute | solution.py:22
  145.7 6.9 %collective-permute-start.1 = (bf16[9,16,256]{2,0,1:T(8,128)(2,1)S(1)}, bf16[9,16,256]{2,0,1:T(8,128)(2,1)S(1)}, u32[]{:S(2)}, u32[]{:S(2)}) collective-permute-start(bf16[9,16,256]{2,0,1:T(8,128)(2,1)S(1)} %get-tuple-element.20), channel_id=1, source_target_pairs={{8,0},{16,8},{24,16},{9,1},{17,9},{25,17},{10,2},{18,10},{26,18},{... | collective-permute-start | bytes 221192 | tf_op jit(solution)/shard_map/ppermute | solution.py:23
  153.2 14.6 %collective-permute-start.2 = (bf16[146,9,256]{2,0,1:T(8,128)(2,1)S(1)}, bf16[146,9,256]{2,0,1:T(8,128)(2,1)S(1)}, u32[]{:S(2)}, u32[]{:S(2)}) collective-permute-start(bf16[146,9,256]{2,0,1:T(8,128)(2,1)S(1)} %get-tuple-element.17), channel_id=1, source_target_pairs={{0,1},{1,2},{2,3},{3,4},{4,5},{5,6},{6,7},{8,9},{9,10},{10,11},{11... | collective-permute-start | bytes 2018312 | tf_op jit(solution)/shard_map/ppermute | solution.py:22
  159.8 12.4 %collective-permute-start.3 = (bf16[146,9,256]{2,0,1:T(8,128)(2,1)S(1)}, bf16[146,9,256]{2,0,1:T(8,128)(2,1)S(1)}, u32[]{:S(2)}, u32[]{:S(2)}) collective-permute-start(bf16[146,9,256]{2,0,1:T(8,128)(2,1)S(1)} %get-tuple-element.18), channel_id=1, source_target_pairs={{1,0},{2,1},{3,2},{4,3},{5,4},{6,5},{7,6},{9,8},{10,9},{11,10},{12... | collective-permute-start | bytes 2018312 | tf_op jit(solution)/shard_map/ppermute | solution.py:23
